TPU v7x, 32 devices: a whole 2x2x4 slice. The times are simulated.
32 devices in a mesh: gx: 4 (over y, x), gy: 2 (over core), gz: 4 (over z).
Axes of the slice: x: 2, y: 2, z: 4, core: 2. Of those that a mesh axis runs over, the one named last changes fastest.
Arguments:
- correction: float32 [64, 64, 512], P('gz', 'gx', 'gy'), may hold values from -6 to 6
- residual: float32 [64, 64, 512], P('gz', 'gx', 'gy'), may hold values from -4 to 6
- state: float32 [64, 64, 512], P('gz', 'gx', 'gy'), may hold values from -1 to 1
- spacing_level: int32 [64], replicated, may hold values from 0 to 3
- line_colour: int32 [64, 512], P('gx', 'gy'), may hold values from 0 to 1
Outputs:
- smoothed: float32 [64, 64, 512], P('gz', 'gx', 'gy')
All inputs are finite; a program needn't handle non-finite values.
Results may differ from a plain program's by a relative error of at most 0.0003.
Values sent between devices are 32-bit elements; how exact they have to be, the bound alone decides.
A program may use at most 64 MiB of HBM per device.

v0:
```python
import jax
import jax.numpy as jnp
from jax import lax
from jax.sharding import PartitionSpec as P

coef_z = 1000.0
coef_x = 0.3
coef_y = 0.2
bratu_lambda = 0.2


def extended(block, sides, width):
    for axis, dim in sides:
        count = lax.axis_size(axis)
        forward = [(i, i + 1) for i in range(count - 1)]
        backward = [(target, source) for source, target in forward]
        low = lax.ppermute(
            lax.slice_in_dim(block, block.shape[dim] - width, None, axis=dim), axis, forward
        )
        high = lax.ppermute(lax.slice_in_dim(block, 0, width, axis=dim), axis, backward)
        block = jnp.concatenate([low, block, high], axis=dim)
    return block


def face_coupling(spacing_level):
    spacing_cells = 0.8 * jnp.power(1.3, spacing_level.astype(jnp.float32))
    inner_faces = coef_z * 2.0 / (spacing_cells[:-1] + spacing_cells[1:])
    nothing = jnp.zeros((1,), jnp.float32)
    face_low = jnp.concatenate([nothing, inner_faces])
    face_high = jnp.concatenate([inner_faces, nothing])
    return (spacing_cells, face_low, face_high)


def move_rows(values, stride, filler):
    length = values.shape[0]
    padding = jnp.full((abs(stride),) + values.shape[1:], filler, values.dtype)
    if stride > 0:
        return jnp.concatenate([padding, values[: length - stride]], 0)
    return jnp.concatenate([values[-stride:], padding], 0)


def factor_local(below_coef, centre, above_coef):
    length = centre.shape[0]
    sections = []
    stride = 1
    while stride < length:
        before_low = move_rows(below_coef, stride, 0.0)
        before_mid = move_rows(centre, stride, 1.0)
        before_high = move_rows(above_coef, stride, 0.0)
        beyond_low = move_rows(below_coef, -stride, 0.0)
        beyond_mid = move_rows(centre, -stride, 1.0)
        beyond_high = move_rows(above_coef, -stride, 0.0)
        weight_low = -below_coef / before_mid
        weight_high = -above_coef / beyond_mid
        centre = centre + weight_low * before_high + weight_high * beyond_low
        below_coef = weight_low * before_low
        above_coef = weight_high * beyond_high
        sections.append((weight_low, weight_high))
        stride = stride * 2
    return (sections, centre)


def apply_local(source, sections, centre):
    stride = 1
    for weight_low, weight_high in sections:
        source = (
            source
            + weight_low * move_rows(source, stride, 0.0)
            + weight_high * move_rows(source, -stride, 0.0)
        )
        stride = stride * 2
    return source / centre


def on_device(correction, residual, state, spacing_level, line_colour):
    depth = correction.shape[0]
    device_place = lax.axis_index("gz")
    spacing_all, face_low_all, face_high_all = face_coupling(spacing_level)
    offset_rows = device_place * depth
    spacing_cells = lax.dynamic_slice_in_dim(spacing_all, offset_rows, depth)
    face_low = lax.dynamic_slice_in_dim(face_low_all, offset_rows, depth)
    face_high = lax.dynamic_slice_in_dim(face_high_all, offset_rows, depth)
    column = spacing_cells[:, None, None]
    centre = (face_low + face_high)[:, None, None] + column * (
        2.0 * coef_x + 2.0 * coef_y - bratu_lambda * jnp.exp(state)
    )
    line_shape = centre.shape
    row_column = jnp.arange(depth)[:, None, None]
    edge_rows = (row_column == 0) | (row_column == depth - 1)
    low_full = jnp.broadcast_to((-face_low)[:, None, None], line_shape)
    high_full = jnp.broadcast_to((-face_high)[:, None, None], line_shape)
    inner_low = jnp.where((row_column <= 1) | (row_column == depth - 1), 0.0, low_full)
    inner_high = jnp.where((row_column >= depth - 2) | (row_column == 0), 0.0, high_full)
    inner_centre = jnp.where(edge_rows, 1.0, centre)
    sections_local, centre_local = factor_local(inner_low, inner_centre, inner_high)
    from_first = apply_local(
        jnp.where(row_column == 1, -low_full, 0.0), sections_local, centre_local
    )
    from_last = apply_local(
        jnp.where(row_column == depth - 2, -high_full, 0.0), sections_local, centre_local
    )
    first_low = low_full[0]
    first_mid = centre[0] + high_full[0] * from_first[1]
    first_high = high_full[0] * from_last[1]
    last_low = low_full[depth - 1] * from_first[depth - 2]
    last_mid = centre[depth - 1] + low_full[depth - 1] * from_last[depth - 2]
    last_high = high_full[depth - 1]
    coupled = jnp.stack(
        [
            jnp.stack([first_low, last_low], 0),
            jnp.stack([first_mid, last_mid], 0),
            jnp.stack([first_high, last_high], 0),
        ],
        0,
    )
    gathered = lax.all_gather(coupled, "gz", axis=1, tiled=True)
    sections_reduced, centre_reduced = factor_local(gathered[0], gathered[1], gathered[2])
    iterate = correction
    for colour in range(2):
        padded = extended(iterate, (("gx", 1), ("gy", 2)), 1)
        beside = coef_x * (padded[:, 2:, 1:-1] + padded[:, :-2, 1:-1]) + coef_y * (
            padded[:, 1:-1, 2:] + padded[:, 1:-1, :-2]
        )
        source = column * (residual + beside)
        interior = apply_local(jnp.where(edge_rows, 0.0, source), sections_local, centre_local)
        first_source = source[0] - high_full[0] * interior[1]
        last_source = source[depth - 1] - low_full[depth - 1] * interior[depth - 2]
        source_pair = jnp.stack([first_source, last_source], 0)
        all_sources = lax.all_gather(source_pair, "gz", axis=0, tiled=True)
        solution = apply_local(all_sources, sections_reduced, centre_reduced)
        ends_value = lax.dynamic_slice_in_dim(solution, 2 * device_place, 2, 0)
        first_cell = ends_value[0]
        last_cell = ends_value[1]
        inside = interior + from_first * first_cell[None] + from_last * last_cell[None]
        solved = jnp.where(
            row_column == 0,
            first_cell[None],
            jnp.where(row_column == depth - 1, last_cell[None], inside),
        )
        iterate = jnp.where((line_colour == colour)[None], solved, iterate)
    return iterate


def solution(mesh):
    return jax.shard_map(
        on_device,
        mesh=mesh,
        in_specs=(
            P("gz", "gx", "gy"),
            P("gz", "gx", "gy"),
            P("gz", "gx", "gy"),
            P(),
            P("gx", "gy"),
        ),
        out_specs=P("gz", "gx", "gy"),
        check_vma=False,
    )
```

profile of v0, /device:TPU:12, one launch (start us, length us, event | category | flops | bytes accessed | tf_op | source)
XLA Modules:
  0.0 85.7 jit_solution(15522667361424550462)
XLA Ops:
  0.0 1.0 %fusion.55 = (f32[16,1,256]{2,1,0:T(1,128)S(1)}, f32[16,1,256]{2,1,0:T(1,128)S(1)}) fusion(f32[16,16,256]{2,1,0:T(8,128)} %param.5), kind=kLoop, calls=%fused_computation.170 | loop fusion | bytes 65536 | tf_op jit(solution)/shard_map/slice | solution.py:18
  1.0 3.3 %collective-permute-start = (f32[16,1,256]{2,1,0:T(1,128)S(1)}, f32[16,1,256]{2,1,0:T(1,128)S(1)}, u32[]{:S(2)}, u32[]{:S(2)}) collective-permute-start(f32[16,1,256]{2,1,0:T(1,128)S(1)} %get-tuple-element.94), channel_id=1, source_target_pairs={{8,0},{16,8},{24,16},{9,1},{17,9},{25,17},{10,2},{18,10},{26,18},{... | collective-permute-start | bytes 49160 | tf_op jit(solution)/shard_map/ppermute | solution.py:20
  4.3 2.5 %collective-permute-start.1 = (f32[16,1,256]{2,1,0:T(1,128)S(1)}, f32[16,1,256]{2,1,0:T(1,128)S(1)}, u32[]{:S(2)}, u32[]{:S(2)}) collective-permute-start(f32[16,1,256]{2,1,0:T(1,128)S(1)} %get-tuple-element.93), channel_id=1, source_target_pairs={{0,8},{8,16},{16,24},{1,9},{9,17},{17,25},{2,10},{10,18},{18,26},{... | collective-permute-start | bytes 49160 | tf_op jit(solution)/shard_map/ppermute | solution.py:17
  6.9 0.6 copy-done.4
  7.6 0.1 pad_maximum_fusion.22
  7.7 0.1 fusion.41
  7.9 0.1 broadcast_select_fusion.1
  8.0 0.1 broadcast_select_fusion
  8.2 0.6 fusion.83
  8.8 0.6 fusion.84
  9.5 1.4 %collective-permute-done.1 = f32[16,1,256]{2,1,0:T(1,128)S(1)} collective-permute-done((f32[16,1,256]{2,1,0:T(1,128)S(1)}, f32[16,1,256]{2,1,0:T(1,128)S(1)}, u32[]{:S(2)}, u32[]{:S(2)}) %collective-permute-start.1) | collective-permute-done | bytes 16416 | tf_op jit(solution)/shard_map/ppermute | solution.py:17
  11.0 0.1 fusion.44
  11.1 1.4 %collective-permute-start.2 = (f32[16,18,1]{2,1,0:T(8,128)S(1)}, f32[16,18,1]{2,1,0:T(8,128)S(1)}, u32[]{:S(2)}, u32[]{:S(2)}) collective-permute-start(f32[16,18,1]{2,1,0:T(8,128)S(1)} %get-tuple-element.63), channel_id=1, source_target_pairs={{4,0},{5,1},{6,2},{7,3},{12,8},{13,9},{14,10},{15,11},{20,16},{21,... | collective-permute-start | bytes 3464 | tf_op jit(solution)/shard_map/ppermute | solution.py:20
  12.5 3.0 %collective-permute-start.3 = (f32[16,18,1]{2,1,0:T(8,128)S(1)}, f32[16,18,1]{2,1,0:T(8,128)S(1)}, u32[]{:S(2)}, u32[]{:S(2)}) collective-permute-start(f32[16,18,1]{2,1,0:T(8,128)S(1)} %get-tuple-element.64), channel_id=1, source_target_pairs={{0,4},{1,5},{2,6},{3,7},{8,12},{9,13},{10,14},{11,15},{16,20},{17,... | collective-permute-start | bytes 3464 | tf_op jit(solution)/shard_map/ppermute | solution.py:17
  15.6 0.1 dynamic_slice.15
  15.7 0.9 %collective-permute-done.3 = f32[16,18,1]{2,1,0:T(8,128)S(1)} collective-permute-done((f32[16,18,1]{2,1,0:T(8,128)S(1)}, f32[16,18,1]{2,1,0:T(8,128)S(1)}, u32[]{:S(2)}, u32[]{:S(2)}) %collective-permute-start.3) | collective-permute-done | bytes 1184 | tf_op jit(solution)/shard_map/ppermute | solution.py:17
  16.6 0.4 broadcast_select_fusion.6
  17.1 0.2 broadcast_select_fusion.2
  17.3 0.2 multiply_add_fusion.5
  17.7 0.3 multiply_add_fusion.7
  18.1 0.1 multiply_add_fusion.12
  18.4 0.5 multiply_add_fusion.13
  19.1 0.3 multiply_add_fusion.11
  19.5 0.3 add_divide_fusion.2
  19.8 1.2 %slice_multiply_fusion.5 = (f32[1,16,256]{2,1,0:T(8,128)S(1)}, f32[1,16,256]{2,1,0:T(8,128)S(1)}, f32[1,16,256]{2,1,0:T(8,128)S(1)}, f32[1,16,256]{2,1,0:T(8,128)S(1)}) fusion(f32[16,16,256]{2,1,0:T(8,128)S(1)} %get-tuple-element.36, f32[]{:T(128)} %bitcast.1, f32[]{:T(128)} %bitcast, f32[16,16,256]{2,1,0:T(8,128)S(1)} %get-tuple-element.158, ...), kind=kLoop, calls=%fused_computation.138 | loop fusion | flops 24576 | bytes 163848 | tf_op jit(solution)/shard_map/mul | solution.py:105
  21.1 0.7 pad_bitcast_fusion.1
  21.7 0.6 pad_bitcast_fusion
  22.4 15.6 %all_gather.10 = f32[3,8,16,256]{3,2,1,0:T(8,128)S(1)} all-gather(f32[3,2,16,256]{3,2,1,0:T(8,128)S(1)} %pad_maximum_fusion.18), channel_id=1, replica_groups=mesh['gx'=4,'gy'=2,'gz'=4] {'gz'}, dimensions={1}, use_global_device_ids=true | all-gather | bytes 491520 | tf_op jit(solution)/shard_map/all_gather | solution.py:116
  38.1 0.2 add_divide_fusion.3
  38.3 1.2 %fusion.35 = (f32[1,16,256]{2,1,0:T(8,128)S(1)}, f32[1,16,256]{2,1,0:T(8,128)S(1)}) fusion(f32[16,16,256]{2,1,0:T(8,128)S(1)} %add_divide_fusion.3, f32[16,16,256]{2,1,0:T(8,128)S(1)} %get-tuple-element.29, f32[]{:T(128)} %bitcast, f32[]{:T(128)} %bitcast.1), kind=kLoop, calls=%fused_computation.142 | loop fusion | flops 16384 | bytes 98312 | tf_op jit(solution)/shard_map/sub | solution.py:126
  39.5 13.5 %all_gather.9 = f32[8,16,256]{2,1,0:T(8,128)S(1)} all-gather(f32[2,16,256]{2,1,0:T(8,128)S(1)} %pad_maximum_fusion.19), channel_id=1, replica_groups=mesh['gx'=4,'gy'=2,'gz'=4] {'gz'}, dimensions={0}, use_global_device_ids=true | all-gather | bytes 163840 | tf_op jit(solution)/shard_map/all_gather | solution.py:129
  53.4 0.1 multiply_add_fusion.20
  53.7 0.1 select_select_fusion.1
  53.8 2.9 %collective-permute-start.4 = (f32[16,1,256]{2,1,0:T(1,128)S(1)}, f32[16,1,256]{2,1,0:T(1,128)S(1)}, u32[]{:S(2)}, u32[]{:S(2)}) collective-permute-start(f32[16,1,256]{2,1,0:T(1,128)S(1)} %get-tuple-element.74), channel_id=1, source_target_pairs={{8,0},{16,8},{24,16},{9,1},{17,9},{25,17},{10,2},{18,10},{26,18},{... | collective-permute-start | bytes 49160 | tf_op jit(solution)/shard_map/ppermute | solution.py:20
  56.7 2.9 %collective-permute-start.5 = (f32[16,1,256]{2,1,0:T(1,128)S(1)}, f32[16,1,256]{2,1,0:T(1,128)S(1)}, u32[]{:S(2)}, u32[]{:S(2)}) collective-permute-start(f32[16,1,256]{2,1,0:T(1,128)S(1)} %get-tuple-element.73), channel_id=1, source_target_pairs={{0,8},{8,16},{16,24},{1,9},{9,17},{17,25},{2,10},{10,18},{18,26},{... | collective-permute-start | bytes 49160 | tf_op jit(solution)/shard_map/ppermute | solution.py:17
  59.7 3.6 %collective-permute-done.5 = f32[16,1,256]{2,1,0:T(1,128)S(1)} collective-permute-done((f32[16,1,256]{2,1,0:T(1,128)S(1)}, f32[16,1,256]{2,1,0:T(1,128)S(1)}, u32[]{:S(2)}, u32[]{:S(2)}) %collective-permute-start.5) | collective-permute-done | bytes 16416 | tf_op jit(solution)/shard_map/ppermute | solution.py:17
  63.3 0.1 fusion.43
  63.4 1.3 %collective-permute-start.6 = (f32[16,18,1]{2,1,0:T(8,128)S(1)}, f32[16,18,1]{2,1,0:T(8,128)S(1)}, u32[]{:S(2)}, u32[]{:S(2)}) collective-permute-start(f32[16,18,1]{2,1,0:T(8,128)S(1)} %get-tuple-element.55), channel_id=1, source_target_pairs={{4,0},{5,1},{6,2},{7,3},{12,8},{13,9},{14,10},{15,11},{20,16},{21,... | collective-permute-start | bytes 3464 | tf_op jit(solution)/shard_map/ppermute | solution.py:20
  64.7 3.0 %collective-permute-start.7 = (f32[16,18,1]{2,1,0:T(8,128)S(1)}, f32[16,18,1]{2,1,0:T(8,128)S(1)}, u32[]{:S(2)}, u32[]{:S(2)}) collective-permute-start(f32[16,18,1]{2,1,0:T(8,128)S(1)} %get-tuple-element.56), channel_id=1, source_target_pairs={{0,4},{1,5},{2,6},{3,7},{8,12},{9,13},{10,14},{11,15},{16,20},{17,... | collective-permute-start | bytes 3464 | tf_op jit(solution)/shard_map/ppermute | solution.py:17
  67.8 1.0 %collective-permute-done.7 = f32[16,18,1]{2,1,0:T(8,128)S(1)} collective-permute-done((f32[16,18,1]{2,1,0:T(8,128)S(1)}, f32[16,18,1]{2,1,0:T(8,128)S(1)}, u32[]{:S(2)}, u32[]{:S(2)}) %collective-permute-start.7) | collective-permute-done | bytes 1184 | tf_op jit(solution)/shard_map/ppermute | solution.py:17
  68.8 0.4 broadcast_select_fusion.5
  69.3 0.2 multiply_add_fusion.2
  69.5 0.1 multiply_add_fusion.1
  69.6 0.1 multiply_add_fusion
  69.8 0.2 add_divide_fusion
  70.0 1.2 %fusion.31 = (f32[1,16,256]{2,1,0:T(8,128)S(1)}, f32[1,16,256]{2,1,0:T(8,128)S(1)}) fusion(f32[16,16,256]{2,1,0:T(8,128)S(1)} %add_divide_fusion, f32[16,16,256]{2,1,0:T(8,128)S(1)} %get-tuple-element.6, f32[]{:T(128)} %bitcast, f32[]{:T(128)} %bitcast.1), kind=kLoop, calls=%fused_computation.130 | loop fusion | flops 16384 | bytes 98312 | tf_op jit(solution)/shard_map/sub | solution.py:126
  71.2 13.4 %all_gather.11 = f32[8,16,256]{2,1,0:T(8,128)S(1)} all-gather(f32[2,16,256]{2,1,0:T(8,128)S(1)} %pad_maximum_fusion.20), channel_id=1, replica_groups=mesh['gx'=4,'gy'=2,'gz'=4] {'gz'}, dimensions={0}, use_global_device_ids=true | all-gather | bytes 163840 | tf_op jit(solution)/shard_map/all_gather | solution.py:129
  84.9 0.8 select_select_fusion
  (82 shorter events, 2.0 us)
Async XLA Ops:
  1.0 8.5 %collective-permute-start = (f32[16,1,256]{2,1,0:T(1,128)S(1)}, f32[16,1,256]{2,1,0:T(1,128)S(1)}, u32[]{:S(2)}, u32[]{:S(2)}) collective-permute-start(f32[16,1,256]{2,1,0:T(1,128)S(1)} %get-tuple-element.94), channel_id=1, source_target_pairs={{8,0},{16,8},{24,16},{9,1},{17,9},{25,17},{10,2},{18,10},{26,18},{... | collective-permute-start | bytes 49160 | tf_op jit(solution)/shard_map/ppermute | solution.py:20
  4.3 6.5 %collective-permute-start.1 = (f32[16,1,256]{2,1,0:T(1,128)S(1)}, f32[16,1,256]{2,1,0:T(1,128)S(1)}, u32[]{:S(2)}, u32[]{:S(2)}) collective-permute-start(f32[16,1,256]{2,1,0:T(1,128)S(1)} %get-tuple-element.93), channel_id=1, source_target_pairs={{0,8},{8,16},{16,24},{1,9},{9,17},{17,25},{2,10},{10,18},{18,26},{... | collective-permute-start | bytes 49160 | tf_op jit(solution)/shard_map/ppermute | solution.py:17
  6.9 0.7 copy-start.4
  8.2 1.3 %copy-start.3 = (s32[16,256]{1,0:T(8,128)S(1)}, s32[16,256]{1,0:T(8,128)}, u32[]{:S(2)}) copy-start(s32[16,256]{1,0:T(8,128)} %param.9) | copy-start | bytes 49156
  8.2 2.7 %copy-start = (f32[16,16,256]{2,1,0:T(8,128)S(1)}, f32[16,16,256]{2,1,0:T(8,128)}, u32[]{:S(2)}) copy-start(f32[16,16,256]{2,1,0:T(8,128)} %param.5) | copy-start | bytes 786436
  10.9 5.7 %copy-start.1 = (f32[16,16,256]{2,1,0:T(8,128)S(1)}, f32[16,16,256]{2,1,0:T(8,128)}, u32[]{:S(2)}) copy-start(f32[16,16,256]{2,1,0:T(8,128)} %param.6) | copy-start | bytes 786436
  11.0 5.7 %copy-start.2 = (f32[16,16,256]{2,1,0:T(8,128)S(1)}, f32[16,16,256]{2,1,0:T(8,128)}, u32[]{:S(2)}) copy-start(f32[16,16,256]{2,1,0:T(8,128)} %param.7) | copy-start | bytes 786436
  11.1 4.6 %collective-permute-start.2 = (f32[16,18,1]{2,1,0:T(8,128)S(1)}, f32[16,18,1]{2,1,0:T(8,128)S(1)}, u32[]{:S(2)}, u32[]{:S(2)}) collective-permute-start(f32[16,18,1]{2,1,0:T(8,128)S(1)} %get-tuple-element.63), channel_id=1, source_target_pairs={{4,0},{5,1},{6,2},{7,3},{12,8},{13,9},{14,10},{15,11},{20,16},{21,... | collective-permute-start | bytes 3464 | tf_op jit(solution)/shard_map/ppermute | solution.py:20
  12.5 4.1 %collective-permute-start.3 = (f32[16,18,1]{2,1,0:T(8,128)S(1)}, f32[16,18,1]{2,1,0:T(8,128)S(1)}, u32[]{:S(2)}, u32[]{:S(2)}) collective-permute-start(f32[16,18,1]{2,1,0:T(8,128)S(1)} %get-tuple-element.64), channel_id=1, source_target_pairs={{0,4},{1,5},{2,6},{3,7},{8,12},{9,13},{10,14},{11,15},{16,20},{17,... | collective-permute-start | bytes 3464 | tf_op jit(solution)/shard_map/ppermute | solution.py:17
  53.8 5.9 %collective-permute-start.4 = (f32[16,1,256]{2,1,0:T(1,128)S(1)}, f32[16,1,256]{2,1,0:T(1,128)S(1)}, u32[]{:S(2)}, u32[]{:S(2)}) collective-permute-start(f32[16,1,256]{2,1,0:T(1,128)S(1)} %get-tuple-element.74), channel_id=1, source_target_pairs={{8,0},{16,8},{24,16},{9,1},{17,9},{25,17},{10,2},{18,10},{26,18},{... | collective-permute-start | bytes 49160 | tf_op jit(solution)/shard_map/ppermute | solution.py:20
  56.7 6.5 %collective-permute-start.5 = (f32[16,1,256]{2,1,0:T(1,128)S(1)}, f32[16,1,256]{2,1,0:T(1,128)S(1)}, u32[]{:S(2)}, u32[]{:S(2)}) collective-permute-start(f32[16,1,256]{2,1,0:T(1,128)S(1)} %get-tuple-element.73), channel_id=1, source_target_pairs={{0,8},{8,16},{16,24},{1,9},{9,17},{17,25},{2,10},{10,18},{18,26},{... | collective-permute-start | bytes 49160 | tf_op jit(solution)/shard_map/ppermute | solution.py:17
  63.4 4.4 %collective-permute-start.6 = (f32[16,18,1]{2,1,0:T(8,128)S(1)}, f32[16,18,1]{2,1,0:T(8,128)S(1)}, u32[]{:S(2)}, u32[]{:S(2)}) collective-permute-start(f32[16,18,1]{2,1,0:T(8,128)S(1)} %get-tuple-element.55), channel_id=1, source_target_pairs={{4,0},{5,1},{6,2},{7,3},{12,8},{13,9},{14,10},{15,11},{20,16},{21,... | collective-permute-start | bytes 3464 | tf_op jit(solution)/shard_map/ppermute | solution.py:20
  64.7 4.1 %collective-permute-start.7 = (f32[16,18,1]{2,1,0:T(8,128)S(1)}, f32[16,18,1]{2,1,0:T(8,128)S(1)}, u32[]{:S(2)}, u32[]{:S(2)}) collective-permute-start(f32[16,18,1]{2,1,0:T(8,128)S(1)} %get-tuple-element.56), channel_id=1, source_target_pairs={{0,4},{1,5},{2,6},{3,7},{8,12},{9,13},{10,14},{11,15},{16,20},{17,... | collective-permute-start | bytes 3464 | tf_op jit(solution)/shard_map/ppermute | solution.py:17
where the time goes:
time: 86.1 us; the launch traced here: 85.7 us
  blocking collectives  42.6 us (49%)
  starting transfers between devices  20.5 us (24%)
  other arithmetic  9.26 us (11%)
  waiting for transfers between devices  6.93 us (8%)
  local copies, waits for them, and re-layouts  5.68 us (7%)
    all_gather x2, blocking collectives, on_device(): all_sources = lax.all_gather(source_pair, 'gz', axis=0, tiled=True)  26.9 us
    all_gather x1, blocking collectives, on_device(): gathered = lax.all_gather(coupled, 'gz', axis=1, tiled=True)  15.6 us
    ppermute x4, starting transfers between devices, extended(): lax.ppermute(lax.slice_in_dim(block, block.shape[dim] - width, None, axis...  11.5 us
    ppermute x4, starting transfers between devices, extended(): lax.ppermute(lax.slice_in_dim(block, 0, width, axis=dim), axis, backward)  8.96 us
    ppermute x4, waiting for transfers between devices, extended(): lax.ppermute(lax.slice_in_dim(block, block.shape[dim] - width, None, axis...  6.92 us
    sub x2, other arithmetic, on_device(): first_source = source[0] - high_full[0] * interior[1]  2.43 us
    add x10, other arithmetic, apply_local(): source + weight_low * move_rows(source, stride, 0.0)  1.9 us
  transfers between devices with their start and end apart: 8, of which 4 were waited for; matrix products, arithmetic and copies ran while one was open for 2% of the time, Pallas kernels for 0%

commit v1 on v0

--- a/solution.py
+++ b/solution.py
@@ -113,7 +113,12 @@
         ],
         0,
     )
-    gathered = lax.all_gather(coupled, "gz", axis=1, tiled=True)
+    ring = [coupled]
+    for hop in range(3):
+        ring.append(lax.ppermute(ring[-1], "gz", [(dev, (dev + 1) % 4) for dev in range(4)]))
+    gathered = jnp.roll(
+        jnp.concatenate(ring[::-1], axis=1), (lax.axis_index("gz") + 1) * ring[0].shape[1], axis=1
+    )
     sections_reduced, centre_reduced = factor_local(gathered[0], gathered[1], gathered[2])
     iterate = correction
     for colour in range(2):

time: 86.1 us -> 81.9 us (0.951)
  the two profiles are of different devices: /device:TPU:12 before, /device:TPU:4 now
where the time goes in v1:
time: 81.9 us; the launch traced here: 81.6 us
  blocking collectives  27.1 us (33%)
  starting transfers between devices  22.3 us (27%)
  waiting for transfers between devices  16.3 us (20%)
  other arithmetic  9.31 us (11%)
  local copies, waits for them, and re-layouts  5.63 us (7%)
  between operations  0.82 us (1%)
    all_gather x2, blocking collectives, on_device(): all_sources = lax.all_gather(source_pair, 'gz', axis=0, tiled=True)  27.1 us
    ppermute x4, starting transfers between devices, extended(): lax.ppermute(lax.slice_in_dim(block, block.shape[dim] - width, None, axis...  9.8 us
    ppermute x4, starting transfers between devices, extended(): lax.ppermute(lax.slice_in_dim(block, 0, width, axis=dim), axis, backward)  8.95 us
    ppermute x3, waiting for transfers between devices, on_device(): lax.ppermute(ring[-1], 'gz', [(dev, (dev + 1) % 4) for dev in range(4)])  8.35 us
    ppermute x4, waiting for transfers between devices, extended(): lax.ppermute(lax.slice_in_dim(block, block.shape[dim] - width, None, axis...  5.95 us
    ppermute x3, starting transfers between devices, on_device(): lax.ppermute(ring[-1], 'gz', [(dev, (dev + 1) % 4) for dev in range(4)])  3.58 us
    sub x2, other arithmetic, on_device(): first_source = source[0] - high_full[0] * interior[1]  2.45 us
    ppermute x4, waiting for transfers between devices, extended(): lax.ppermute(lax.slice_in_dim(block, 0, width, axis=dim), axis, backward)  2.03 us
  transfers between devices with their start and end apart: 11, of which 6 were waited for; matrix products, arithmetic and copies ran while one was open for 4% of the time, Pallas kernels for 0%

profile of v1, /device:TPU:4, one launch (start us, length us, event | category | flops | bytes accessed | tf_op | source)
XLA Modules:
  0.0 81.6 jit_solution(6691374906991897618)
XLA Ops:
  0.0 1.0 %fusion.55 = (f32[16,1,256]{2,1,0:T(1,128)S(1)}, f32[16,1,256]{2,1,0:T(1,128)S(1)}) fusion(f32[16,16,256]{2,1,0:T(8,128)} %param.5), kind=kLoop, calls=%fused_computation.178 | loop fusion | bytes 65536 | tf_op jit(solution)/shard_map/slice | solution.py:18
  1.0 3.3 %collective-permute-start = (f32[16,1,256]{2,1,0:T(1,128)S(1)}, f32[16,1,256]{2,1,0:T(1,128)S(1)}, u32[]{:S(2)}, u32[]{:S(2)}) collective-permute-start(f32[16,1,256]{2,1,0:T(1,128)S(1)} %get-tuple-element.94), channel_id=1, source_target_pairs={{8,0},{16,8},{24,16},{9,1},{17,9},{25,17},{10,2},{18,10},{26,18},{... | collective-permute-start | bytes 49160 | tf_op jit(solution)/shard_map/ppermute | solution.py:20
  4.3 2.5 %collective-permute-start.1 = (f32[16,1,256]{2,1,0:T(1,128)S(1)}, f32[16,1,256]{2,1,0:T(1,128)S(1)}, u32[]{:S(2)}, u32[]{:S(2)}) collective-permute-start(f32[16,1,256]{2,1,0:T(1,128)S(1)} %get-tuple-element.93), channel_id=1, source_target_pairs={{0,8},{8,16},{16,24},{1,9},{9,17},{17,25},{2,10},{10,18},{18,26},{... | collective-permute-start | bytes 49160 | tf_op jit(solution)/shard_map/ppermute | solution.py:17
  6.9 0.6 copy-done.4
  7.9 0.1 broadcast_select_fusion.1
  8.1 0.1 broadcast_select_fusion
  8.2 0.6 fusion.83
  8.8 0.6 fusion.84
  9.5 1.4 %collective-permute-done.1 = f32[16,1,256]{2,1,0:T(1,128)S(1)} collective-permute-done((f32[16,1,256]{2,1,0:T(1,128)S(1)}, f32[16,1,256]{2,1,0:T(1,128)S(1)}, u32[]{:S(2)}, u32[]{:S(2)}) %collective-permute-start.1) | collective-permute-done | bytes 16416 | tf_op jit(solution)/shard_map/ppermute | solution.py:17
  11.0 0.1 fusion.44
  11.1 1.4 %collective-permute-start.2 = (f32[16,18,1]{2,1,0:T(8,128)S(1)}, f32[16,18,1]{2,1,0:T(8,128)S(1)}, u32[]{:S(2)}, u32[]{:S(2)}) collective-permute-start(f32[16,18,1]{2,1,0:T(8,128)S(1)} %get-tuple-element.63), channel_id=1, source_target_pairs={{4,0},{5,1},{6,2},{7,3},{12,8},{13,9},{14,10},{15,11},{20,16},{21,... | collective-permute-start | bytes 3464 | tf_op jit(solution)/shard_map/ppermute | solution.py:20
  12.5 3.0 %collective-permute-start.3 = (f32[16,18,1]{2,1,0:T(8,128)S(1)}, f32[16,18,1]{2,1,0:T(8,128)S(1)}, u32[]{:S(2)}, u32[]{:S(2)}) collective-permute-start(f32[16,18,1]{2,1,0:T(8,128)S(1)} %get-tuple-element.64), channel_id=1, source_target_pairs={{0,4},{1,5},{2,6},{3,7},{8,12},{9,13},{10,14},{11,15},{16,20},{17,... | collective-permute-start | bytes 3464 | tf_op jit(solution)/shard_map/ppermute | solution.py:17
  15.6 1.0 %collective-permute-done.3 = f32[16,18,1]{2,1,0:T(8,128)S(1)} collective-permute-done((f32[16,18,1]{2,1,0:T(8,128)S(1)}, f32[16,18,1]{2,1,0:T(8,128)S(1)}, u32[]{:S(2)}, u32[]{:S(2)}) %collective-permute-start.3) | collective-permute-done | bytes 1184 | tf_op jit(solution)/shard_map/ppermute | solution.py:17
  16.6 0.4 broadcast_select_fusion.6
  17.1 0.2 broadcast_select_fusion.2
  17.3 0.2 multiply_add_fusion.5
  17.7 0.3 multiply_add_fusion.7
  18.1 0.1 multiply_add_fusion.12
  18.4 0.5 multiply_add_fusion.13
  19.1 0.3 multiply_add_fusion.11
  19.5 0.3 add_divide_fusion.2
  19.8 1.2 %slice_multiply_fusion.5 = (f32[1,16,256]{2,1,0:T(8,128)S(1)}, f32[1,16,256]{2,1,0:T(8,128)S(1)}, f32[1,16,256]{2,1,0:T(8,128)S(1)}, f32[1,16,256]{2,1,0:T(8,128)S(1)}) fusion(f32[16,16,256]{2,1,0:T(8,128)S(1)} %get-tuple-element.36, f32[]{:T(128)} %bitcast.1, f32[]{:T(128)} %bitcast, f32[16,16,256]{2,1,0:T(8,128)S(1)} %get-tuple-element.158, ...), kind=kLoop, calls=%fused_computation.146 | loop fusion | flops 24576 | bytes 163848 | tf_op jit(solution)/shard_map/mul | solution.py:105
  21.0 0.7 pad_bitcast_fusion.1
  21.7 0.6 pad_bitcast_fusion
  22.4 1.6 %collective-permute-start.4 = (f32[3,2,16,256]{3,2,1,0:T(8,128)S(1)}, f32[3,2,16,256]{3,2,1,0:T(8,128)S(1)}, u32[]{:S(2)}, u32[]{:S(2)}) collective-permute-start(f32[3,2,16,256]{3,2,1,0:T(8,128)S(1)} %pad_maximum_fusion.18), channel_id=1, source_target_pairs={{0,1},{1,2},{2,3},{3,0},{4,5},{5,6},{6,7},{7,4},{8,9},{9,10},{10,1... | collective-permute-start | bytes 294920 | tf_op jit(solution)/shard_map/ppermute | solution.py:118
  24.0 0.2 add_divide_fusion.3
  24.2 1.2 %fusion.35 = (f32[1,16,256]{2,1,0:T(8,128)S(1)}, f32[1,16,256]{2,1,0:T(8,128)S(1)}) fusion(f32[16,16,256]{2,1,0:T(8,128)S(1)} %add_divide_fusion.3, f32[16,16,256]{2,1,0:T(8,128)S(1)} %get-tuple-element.29, f32[]{:T(128)} %bitcast, f32[]{:T(128)} %bitcast.1), kind=kLoop, calls=%fused_computation.150 | loop fusion | flops 16384 | bytes 98312 | tf_op jit(solution)/shard_map/sub | solution.py:131
  25.5 3.9 %collective-permute-done.4 = f32[3,2,16,256]{3,2,1,0:T(8,128)S(1)} collective-permute-done((f32[3,2,16,256]{3,2,1,0:T(8,128)S(1)}, f32[3,2,16,256]{3,2,1,0:T(8,128)S(1)}, u32[]{:S(2)}, u32[]{:S(2)}) %collective-permute-start.4) | collective-permute-done | bytes 98336 | tf_op jit(solution)/shard_map/ppermute | solution.py:118
  29.4 13.8 %all_gather.6 = f32[8,16,256]{2,1,0:T(8,128)S(1)} all-gather(f32[2,16,256]{2,1,0:T(8,128)S(1)} %pad_maximum_fusion.19), channel_id=1, replica_groups=mesh['gx'=4,'gy'=2,'gz'=4] {'gz'}, dimensions={0}, use_global_device_ids=true | all-gather | bytes 163840 | tf_op jit(solution)/shard_map/all_gather | solution.py:134
  43.2 1.9 %collective-permute-start.6 = (f32[3,2,16,256]{3,2,1,0:T(8,128)S(1)}, f32[3,2,16,256]{3,2,1,0:T(8,128)S(1)}, u32[]{:S(2)}, u32[]{:S(2)}) collective-permute-start(f32[3,2,16,256]{3,2,1,0:T(8,128)S(1)} %collective-permute-done.5), channel_id=1, source_target_pairs={{0,1},{1,2},{2,3},{3,0},{4,5},{5,6},{6,7},{7,4},{8,9},{9,10},{10,1... | collective-permute-start | bytes 294920 | tf_op jit(solution)/shard_map/ppermute | solution.py:118
  45.1 4.5 %collective-permute-done.6 = f32[3,2,16,256]{3,2,1,0:T(8,128)S(1)} collective-permute-done((f32[3,2,16,256]{3,2,1,0:T(8,128)S(1)}, f32[3,2,16,256]{3,2,1,0:T(8,128)S(1)}, u32[]{:S(2)}, u32[]{:S(2)}) %collective-permute-start.6) | collective-permute-done | bytes 98336 | tf_op jit(solution)/shard_map/ppermute | solution.py:118
  50.1 0.1 multiply_add_fusion.20
  50.4 0.1 select_select_fusion.1
  50.5 2.9 %collective-permute-start.7 = (f32[16,1,256]{2,1,0:T(1,128)S(1)}, f32[16,1,256]{2,1,0:T(1,128)S(1)}, u32[]{:S(2)}, u32[]{:S(2)}) collective-permute-start(f32[16,1,256]{2,1,0:T(1,128)S(1)} %get-tuple-element.74), channel_id=1, source_target_pairs={{8,0},{16,8},{24,16},{9,1},{17,9},{25,17},{10,2},{18,10},{26,18},{... | collective-permute-start | bytes 49160 | tf_op jit(solution)/shard_map/ppermute | solution.py:20
  53.4 2.9 %collective-permute-start.8 = (f32[16,1,256]{2,1,0:T(1,128)S(1)}, f32[16,1,256]{2,1,0:T(1,128)S(1)}, u32[]{:S(2)}, u32[]{:S(2)}) collective-permute-start(f32[16,1,256]{2,1,0:T(1,128)S(1)} %get-tuple-element.73), channel_id=1, source_target_pairs={{0,8},{8,16},{16,24},{1,9},{9,17},{17,25},{2,10},{10,18},{18,26},{... | collective-permute-start | bytes 49160 | tf_op jit(solution)/shard_map/ppermute | solution.py:17
  56.4 3.6 %collective-permute-done.8 = f32[16,1,256]{2,1,0:T(1,128)S(1)} collective-permute-done((f32[16,1,256]{2,1,0:T(1,128)S(1)}, f32[16,1,256]{2,1,0:T(1,128)S(1)}, u32[]{:S(2)}, u32[]{:S(2)}) %collective-permute-start.8) | collective-permute-done | bytes 16416 | tf_op jit(solution)/shard_map/ppermute | solution.py:17
  60.0 0.1 fusion.43
  60.1 1.3 %collective-permute-start.10 = (f32[16,18,1]{2,1,0:T(8,128)S(1)}, f32[16,18,1]{2,1,0:T(8,128)S(1)}, u32[]{:S(2)}, u32[]{:S(2)}) collective-permute-start(f32[16,18,1]{2,1,0:T(8,128)S(1)} %get-tuple-element.62), channel_id=1, source_target_pairs={{0,4},{1,5},{2,6},{3,7},{8,12},{9,13},{10,14},{11,15},{16,20},{17,... | collective-permute-start | bytes 3464 | tf_op jit(solution)/shard_map/ppermute | solution.py:17
  61.5 1.3 %collective-permute-start.9 = (f32[16,18,1]{2,1,0:T(8,128)S(1)}, f32[16,18,1]{2,1,0:T(8,128)S(1)}, u32[]{:S(2)}, u32[]{:S(2)}) collective-permute-start(f32[16,18,1]{2,1,0:T(8,128)S(1)} %get-tuple-element.61), channel_id=1, source_target_pairs={{4,0},{5,1},{6,2},{7,3},{12,8},{13,9},{14,10},{15,11},{20,16},{21,... | collective-permute-start | bytes 3464 | tf_op jit(solution)/shard_map/ppermute | solution.py:20
  62.8 2.0 %collective-permute-done.9 = f32[16,18,1]{2,1,0:T(8,128)S(1)} collective-permute-done((f32[16,18,1]{2,1,0:T(8,128)S(1)}, f32[16,18,1]{2,1,0:T(8,128)S(1)}, u32[]{:S(2)}, u32[]{:S(2)}) %collective-permute-start.9) | collective-permute-done | bytes 1184 | tf_op jit(solution)/shard_map/ppermute | solution.py:20
  64.8 0.4 broadcast_select_fusion.5
  65.2 0.2 multiply_add_fusion.2
  65.4 0.1 multiply_add_fusion.1
  65.6 0.1 multiply_add_fusion
  65.7 0.2 add_divide_fusion
  65.9 1.2 %fusion.31 = (f32[1,16,256]{2,1,0:T(8,128)S(1)}, f32[1,16,256]{2,1,0:T(8,128)S(1)}) fusion(f32[16,16,256]{2,1,0:T(8,128)S(1)} %add_divide_fusion, f32[16,16,256]{2,1,0:T(8,128)S(1)} %get-tuple-element.6, f32[]{:T(128)} %bitcast, f32[]{:T(128)} %bitcast.1), kind=kLoop, calls=%fused_computation.138 | loop fusion | flops 16384 | bytes 98312 | tf_op jit(solution)/shard_map/sub | solution.py:131
  67.2 13.3 %all_gather.7 = f32[8,16,256]{2,1,0:T(8,128)S(1)} all-gather(f32[2,16,256]{2,1,0:T(8,128)S(1)} %pad_maximum_fusion.20), channel_id=1, replica_groups=mesh['gx'=4,'gy'=2,'gz'=4] {'gz'}, dimensions={0}, use_global_device_ids=true | all-gather | bytes 163840 | tf_op jit(solution)/shard_map/all_gather | solution.py:134
  80.8 0.8 %select_select_fusion = f32[16,16,256]{2,1,0:T(8,128)} fusion(f32[16,16,256]{2,1,0:T(8,128)S(1)} %select_select_fusion.1, f32[16,16,256]{2,1,0:T(8,128)S(1)} %get-tuple-element.37, f32[16,16,256]{2,1,0:T(8,128)S(1)} %add_divide_fusion, f32[16,16,256]{2,1,0:T(8,128)S(1)} %get-tuple-element.36, f32[16,256]{1,0:T(8,128)S(1)} %get-tuple-element.152, ...), kind=kLoop, calls=%fused_computation.32 | loop fusion | flops 458752 | bytes 1347616 | tf_op jit(solution)/shard_map/jit(_where)/select_n | solution.py:145
  (95 shorter events, 2.3 us)
Async XLA Ops:
  1.0 8.5 %collective-permute-start = (f32[16,1,256]{2,1,0:T(1,128)S(1)}, f32[16,1,256]{2,1,0:T(1,128)S(1)}, u32[]{:S(2)}, u32[]{:S(2)}) collective-permute-start(f32[16,1,256]{2,1,0:T(1,128)S(1)} %get-tuple-element.94), channel_id=1, source_target_pairs={{8,0},{16,8},{24,16},{9,1},{17,9},{25,17},{10,2},{18,10},{26,18},{... | collective-permute-start | bytes 49160 | tf_op jit(solution)/shard_map/ppermute | solution.py:20
  4.3 6.5 %collective-permute-start.1 = (f32[16,1,256]{2,1,0:T(1,128)S(1)}, f32[16,1,256]{2,1,0:T(1,128)S(1)}, u32[]{:S(2)}, u32[]{:S(2)}) collective-permute-start(f32[16,1,256]{2,1,0:T(1,128)S(1)} %get-tuple-element.93), channel_id=1, source_target_pairs={{0,8},{8,16},{16,24},{1,9},{9,17},{17,25},{2,10},{10,18},{18,26},{... | collective-permute-start | bytes 49160 | tf_op jit(solution)/shard_map/ppermute | solution.py:17
  6.9 0.7 copy-start.4
  8.2 1.2 %copy-start.3 = (s32[16,256]{1,0:T(8,128)S(1)}, s32[16,256]{1,0:T(8,128)}, u32[]{:S(2)}) copy-start(s32[16,256]{1,0:T(8,128)} %param.9) | copy-start | bytes 49156
  8.2 2.7 %copy-start = (f32[16,16,256]{2,1,0:T(8,128)S(1)}, f32[16,16,256]{2,1,0:T(8,128)}, u32[]{:S(2)}) copy-start(f32[16,16,256]{2,1,0:T(8,128)} %param.5) | copy-start | bytes 786436
  10.9 5.7 %copy-start.1 = (f32[16,16,256]{2,1,0:T(8,128)S(1)}, f32[16,16,256]{2,1,0:T(8,128)}, u32[]{:S(2)}) copy-start(f32[16,16,256]{2,1,0:T(8,128)} %param.6) | copy-start | bytes 786436
  11.0 5.7 %copy-start.2 = (f32[16,16,256]{2,1,0:T(8,128)S(1)}, f32[16,16,256]{2,1,0:T(8,128)}, u32[]{:S(2)}) copy-start(f32[16,16,256]{2,1,0:T(8,128)} %param.7) | copy-start | bytes 786436
  11.1 4.5 %collective-permute-start.2 = (f32[16,18,1]{2,1,0:T(8,128)S(1)}, f32[16,18,1]{2,1,0:T(8,128)S(1)}, u32[]{:S(2)}, u32[]{:S(2)}) collective-permute-start(f32[16,18,1]{2,1,0:T(8,128)S(1)} %get-tuple-element.63), channel_id=1, source_target_pairs={{4,0},{5,1},{6,2},{7,3},{12,8},{13,9},{14,10},{15,11},{20,16},{21,... | collective-permute-start | bytes 3464 | tf_op jit(solution)/shard_map/ppermute | solution.py:20
  12.5 4.1 %collective-permute-start.3 = (f32[16,18,1]{2,1,0:T(8,128)S(1)}, f32[16,18,1]{2,1,0:T(8,128)S(1)}, u32[]{:S(2)}, u32[]{:S(2)}) collective-permute-start(f32[16,18,1]{2,1,0:T(8,128)S(1)} %get-tuple-element.64), channel_id=1, source_target_pairs={{0,4},{1,5},{2,6},{3,7},{8,12},{9,13},{10,14},{11,15},{16,20},{17,... | collective-permute-start | bytes 3464 | tf_op jit(solution)/shard_map/ppermute | solution.py:17
  22.4 7.0 %collective-permute-start.4 = (f32[3,2,16,256]{3,2,1,0:T(8,128)S(1)}, f32[3,2,16,256]{3,2,1,0:T(8,128)S(1)}, u32[]{:S(2)}, u32[]{:S(2)}) collective-permute-start(f32[3,2,16,256]{3,2,1,0:T(8,128)S(1)} %pad_maximum_fusion.18), channel_id=1, source_target_pairs={{0,1},{1,2},{2,3},{3,0},{4,5},{5,6},{6,7},{7,4},{8,9},{9,10},{10,1... | collective-permute-start | bytes 294920 | tf_op jit(solution)/shard_map/ppermute | solution.py:118
  29.3 13.8 %collective-permute-start.5 = (f32[3,2,16,256]{3,2,1,0:T(8,128)S(1)}, f32[3,2,16,256]{3,2,1,0:T(8,128)S(1)}, u32[]{:S(2)}, u32[]{:S(2)}) collective-permute-start(f32[3,2,16,256]{3,2,1,0:T(8,128)S(1)} %collective-permute-done.4), channel_id=1, source_target_pairs={{0,1},{1,2},{2,3},{3,0},{4,5},{5,6},{6,7},{7,4},{8,9},{9,10},{10,1... | collective-permute-start | bytes 294920 | tf_op jit(solution)/shard_map/ppermute | solution.py:118
  43.2 6.4 %collective-permute-start.6 = (f32[3,2,16,256]{3,2,1,0:T(8,128)S(1)}, f32[3,2,16,256]{3,2,1,0:T(8,128)S(1)}, u32[]{:S(2)}, u32[]{:S(2)}) collective-permute-start(f32[3,2,16,256]{3,2,1,0:T(8,128)S(1)} %collective-permute-done.5), channel_id=1, source_target_pairs={{0,1},{1,2},{2,3},{3,0},{4,5},{5,6},{6,7},{7,4},{8,9},{9,10},{10,1... | collective-permute-start | bytes 294920 | tf_op jit(solution)/shard_map/ppermute | solution.py:118
  50.5 5.9 %collective-permute-start.7 = (f32[16,1,256]{2,1,0:T(1,128)S(1)}, f32[16,1,256]{2,1,0:T(1,128)S(1)}, u32[]{:S(2)}, u32[]{:S(2)}) collective-permute-start(f32[16,1,256]{2,1,0:T(1,128)S(1)} %get-tuple-element.74), channel_id=1, source_target_pairs={{8,0},{16,8},{24,16},{9,1},{17,9},{25,17},{10,2},{18,10},{26,18},{... | collective-permute-start | bytes 49160 | tf_op jit(solution)/shard_map/ppermute | solution.py:20
  53.4 6.5 %collective-permute-start.8 = (f32[16,1,256]{2,1,0:T(1,128)S(1)}, f32[16,1,256]{2,1,0:T(1,128)S(1)}, u32[]{:S(2)}, u32[]{:S(2)}) collective-permute-start(f32[16,1,256]{2,1,0:T(1,128)S(1)} %get-tuple-element.73), channel_id=1, source_target_pairs={{0,8},{8,16},{16,24},{1,9},{9,17},{17,25},{2,10},{10,18},{18,26},{... | collective-permute-start | bytes 49160 | tf_op jit(solution)/shard_map/ppermute | solution.py:17
  60.1 2.6 %collective-permute-start.10 = (f32[16,18,1]{2,1,0:T(8,128)S(1)}, f32[16,18,1]{2,1,0:T(8,128)S(1)}, u32[]{:S(2)}, u32[]{:S(2)}) collective-permute-start(f32[16,18,1]{2,1,0:T(8,128)S(1)} %get-tuple-element.62), channel_id=1, source_target_pairs={{0,4},{1,5},{2,6},{3,7},{8,12},{9,13},{10,14},{11,15},{16,20},{17,... | collective-permute-start | bytes 3464 | tf_op jit(solution)/shard_map/ppermute | solution.py:17
  61.5 3.3 %collective-permute-start.9 = (f32[16,18,1]{2,1,0:T(8,128)S(1)}, f32[16,18,1]{2,1,0:T(8,128)S(1)}, u32[]{:S(2)}, u32[]{:S(2)}) collective-permute-start(f32[16,18,1]{2,1,0:T(8,128)S(1)} %get-tuple-element.61), channel_id=1, source_target_pairs={{4,0},{5,1},{6,2},{7,3},{12,8},{13,9},{14,10},{15,11},{20,16},{21,... | collective-permute-start | bytes 3464 | tf_op jit(solution)/shard_map/ppermute | solution.py:20
